TPU v7x, 128 devices: a whole 4x4x4 slice. The times are simulated.
128 devices in a mesh: row: 8 (over y_lo, z), col: 16 (over x, y_hi, core).
Axes of the slice: x: 4, y: 4 (y_hi: 2, y_lo: 2; y = y_hi * 2 + y_lo), z: 4, core: 2. Of those that a mesh axis runs over, the one named last changes fastest.
Arguments:
- inverse: float32 [16384, 16384], P('row', 'col'), may hold values from -0.0625 to 0.0625
- pattern: int32 [128, 128], P('row', 'col'), may hold values 0 or 1
- factor_first: float32 [16384, 256], P('col'), may hold values from -1.5 to 1.5
- factor_second: float32 [16384, 256], P('col'), may hold values from -1.5 to 1.5
- rows_first: int32 [64], replicated, may hold values from 0 to 127, as said below
- rows_second: int32 [64], replicated, may hold values from 0 to 127, as said below
- coupling: float32 [256, 256], replicated, may hold values from -0.375 to 0.375
- diag_first: float32 [256, 256], replicated, may hold values from -6 to 6
- diag_second: float32 [256, 256], replicated, may hold values from -6 to 6
Outputs:
- panel_one: float32 [16384, 256], P(('row', 'col'))
- panel_two: float32 [16384, 256], P(('row', 'col'))
- block_one: float32 [256, 256], replicated
- block_cross: float32 [256, 256], replicated
- block_two: float32 [256, 256], replicated
Inputs may be any that keep to these rules, and one draw needn't show every extreme that they name: `rows_first`: 64 distinct block indices in increasing order; the first block, the block 64 and the last block are always among them. `rows_second`: 64 distinct block indices in increasing order; the first block, the block 64 and the last block are always among them.
All inputs are finite; a program needn't handle non-finite values. No bound on the sum of `pattern` on one device may be relied on, other than what follows from the above.
Results may differ from a plain program's by a relative error of at most 0.000071.
Values sent between devices are 32-bit elements; how exact they have to be, the bound alone decides.
A program may use at most 128 MiB of HBM per device.

v0:
```python
import jax
import jax.numpy as jnp
from jax import lax
from jax.sharding import PartitionSpec as P

BLK = 128


def member(block_ids, rows_list):
    hits = (block_ids[:, None] == rows_list[None, :]).astype(jnp.float32)
    return jnp.sum(hits, axis=1)


def per_device(
    inverse,
    pattern,
    factor_first,
    factor_second,
    rows_first,
    rows_second,
    coupling,
    diag_first,
    diag_second,
):
    high = lax.Precision.HIGHEST
    col_count = lax.axis_size("col")
    row_index = lax.axis_index("row")
    col_index = lax.axis_index("col")
    share_rows = factor_first.shape[0]
    local_rows, local_cols = inverse.shape
    quota_rows = local_rows // col_count
    masked = (
        inverse.reshape(local_rows // BLK, BLK, local_cols // BLK, BLK)
        * pattern.astype(jnp.float32)[:, None, :, None]
    ).reshape(local_rows, local_cols)
    share_ids = (col_index * share_rows + jnp.arange(share_rows, dtype=jnp.int32)) // BLK
    own_start = (row_index * col_count + col_index) * quota_rows
    own_ids = (own_start + jnp.arange(quota_rows, dtype=jnp.int32)) // BLK

    def fetch_rows(factor):
        gathered = lax.all_gather(factor, "col", axis=0, tiled=True)
        return lax.dynamic_slice_in_dim(gathered, own_start, quota_rows, 0)

    def panel_product(factor_kept):
        return lax.psum_scatter(
            jnp.dot(masked, factor_kept, precision=high), "col", scatter_dimension=0, tiled=True
        )

    x_one = factor_first * member(share_ids, rows_first)[:, None]
    x_two = factor_second * member(share_ids, rows_second)[:, None]
    panel_one = -panel_product(x_one)
    near_one = fetch_rows(factor_first)
    near_one = near_one * member(own_ids, rows_first)[:, None]
    first_total = lax.psum(jnp.dot(near_one.T, panel_one, precision=high), ("row", "col"))
    block_one = diag_first - first_total
    near_two = fetch_rows(factor_second)
    near_two = near_two * member(own_ids, rows_second)[:, None]
    panel_two = -(panel_product(x_two) + jnp.dot(panel_one, coupling, precision=high))
    cross_sum, quad_sum = lax.psum(
        (
            jnp.dot(panel_one.T, near_two, precision=high),
            jnp.dot(near_two.T, panel_two, precision=high),
        ),
        ("row", "col"),
    )
    block_cross = -(cross_sum + jnp.dot(block_one, coupling, precision=high))
    block_two = diag_second - quad_sum - jnp.dot(coupling.T, block_cross, precision=high)
    return (panel_one, panel_two, block_one, block_cross, block_two)


def solution(mesh):
    return jax.shard_map(
        per_device,
        mesh=mesh,
        in_specs=(
            P("row", "col"),
            P("row", "col"),
            P("col", None),
            P("col", None),
            P(),
            P(),
            P(),
            P(),
            P(),
        ),
        out_specs=(P(("row", "col"), None), P(("row", "col"), None), P(), P(), P()),
        check_vma=False,
    )
```

profile of v0, /device:TPU:1, one launch (start us, length us, event | category | flops | bytes accessed | tf_op | source)
XLA Modules:
  0.0 555.6 jit_solution(4285565588301605714)
XLA Ops:
  7.2 0.0 copy-start
  7.2 0.0 reduce-scatter.3.cloned.1.call-start
  7.2 0.7 convert_element_type.15
  7.9 0.1 copy.16
  8.0 0.0 copy-start.2
  8.0 1.0 convert_reduce_fusion
  9.0 0.6 mul.52
  9.6 0.0 copy-start.1
  9.6 3.8 copy-done.1
  13.4 0.1 copy-done.2
  13.5 0.0 copy-start.3
  13.5 10.3 %fusion.1 = f32[2048,256]{1,0:T(8,128)} fusion(f32[2048,1024]{1,0:T(8,128)S(1)} %copy-done.2, f32[256,8,8,128]{3,2,1,0:T(8,128)S(1)} %bitcast.19, f32[1024,256]{1,0:T(8,128)} %param.11, f32[1024]{0:T(1024)S(1)} %get-tuple-element.6), kind=kOutput, calls=%fused_computation.2 | convolution fusion | flops 6444810240 | bytes 19927040 | tf_op jit(solution)/shard_map/dot_general | solution.py:46
  23.8 0.0 reduce-scatter.3.cloned.1.call-update
  23.8 0.2 reduce-scatter.5.cloned.1.call-start
  24.0 0.0 copy-done.3
  24.0 0.0 copy-start.10
  24.0 0.0 copy-start.11
  24.1 0.0 copy-start.8
  24.1 12.9 %fusion = f32[2048,256]{1,0:T(8,128)} fusion(f32[2048,1024]{1,0:T(8,128)} %param.9, f32[256,8,8,128]{3,2,1,0:T(8,128)} %bitcast.20, f32[1024,256]{1,0:T(8,128)S(1)} %copy-done.3, f32[1024]{0:T(1024)S(1)} %get-tuple-element.5), kind=kOutput, calls=%fused_computation.1 | convolution fusion | flops 6444810240 | bytes 19927040 | tf_op jit(solution)/shard_map/dot_general | solution.py:46
  36.9 0.0 copy-start.9
  36.9 0.0 reduce-scatter.5.cloned.1.call-update
  37.0 0.0 all-gather.5.cloned.1.call-start
  37.0 0.7 all-gather.5.cloned.1.call-update
  37.7 0.0 all-gather.3.cloned.1.call-start
  37.8 0.5 all-gather.3.cloned.1.call-update
  38.3 0.0 all-reduce.3.cloned.1.call-start
  38.4 0.0 copy-done.10
  38.4 0.0 copy-done.11
  38.4 0.1 convert_reduce_fusion.2
  38.5 57.6 %reduce-scatter.3.cloned.1.call-done = f32[128,256]{1,0:T(8,128)} async-done(((f32[2048,256]{1,0:T(8,128)}), f32[128,256]{1,0:T(8,128)}) %reduce-scatter.3.cloned.1.call-update) | async-done | bytes 131088 | tf_op jit(solution)/shard_map/reduce_scatter | solution.py:45
  96.1 0.9 neg.9
  97.0 0.0 copy-start.4
  97.0 73.0 %reduce-scatter.5.cloned.1.call-done = f32[128,256]{1,0:T(8,128)} async-done(((f32[2048,256]{1,0:T(8,128)}), f32[128,256]{1,0:T(8,128)}) %reduce-scatter.5.cloned.1.call-update) | async-done | bytes 131088 | tf_op jit(solution)/shard_map/reduce_scatter | solution.py:45
  170.0 0.0 copy-done
  170.0 1.2 fusion.4
  171.2 0.0 copy-start.7
  171.2 112.4 %all-gather.5.cloned.1.call-done = f32[16384,256]{1,0:T(8,128)} async-done(((f32[1024,256]{1,0:T(8,128)}), f32[16384,256]{1,0:T(8,128)}) %all-gather.5.cloned.1.call-update) | async-done | bytes 16777232 | tf_op jit(solution)/shard_map/all_gather | solution.py:41
  283.5 2.1 fusion.13
  285.6 2.1 fusion.12
  287.7 105.6 %all-gather.3.cloned.1.call-done = f32[16384,256]{1,0:T(8,128)} async-done(((f32[1024,256]{1,0:T(8,128)}), f32[16384,256]{1,0:T(8,128)}) %all-gather.3.cloned.1.call-update) | async-done | bytes 16777232 | tf_op jit(solution)/shard_map/all_gather | solution.py:41
  393.3 2.1 fusion.9
  395.3 0.0 all-reduce.3.cloned.1.call-update
  395.4 148.9 %all-reduce.3.cloned.1.call-done = (f32[256,256]{1,0:T(8,128)}, f32[256,256]{1,0:T(8,128)}, f32[256,256]{1,0:T(8,128)}) async-done(((f32[256,256]{1,0:T(8,128)}, f32[256,256]{1,0:T(8,128)}, f32[256,256]{1,0:T(8,128)}), (f32[256,256]{1,0:T(8,128)}, f32[256,256]{1,0:T(8,128)}, f32[256,256]{1,0:T(8,128)})) %all-reduce.3.cloned.1.call-update) | async-done | bytes 786448 | tf_op jit(solution)/shard_map/psum | solution.py:54
  544.3 0.0 copy-done.8
  544.3 1.0 sub.23
  545.2 0.0 copy-start.5
  545.3 1.4 fusion.3
  546.7 0.0 copy-start.6
  546.7 0.0 copy-done.9
  546.7 2.3 fusion.2
  549.1 0.0 copy-done.4
  549.1 0.0 copy-done.7
  549.1 0.0 copy-done.5
  549.1 0.0 copy-done.6
  (2 shorter events, 0.0 us)
Async XLA Ops:
  7.2 162.8 %copy-start = (f32[256,256]{1,0:T(8,128)S(1)}, f32[256,256]{1,0:T(8,128)}, u32[]{:S(2)}) copy-start(f32[256,256]{1,0:T(8,128)} %param.15) | copy-start | bytes 786436
  7.2 88.9 %reduce-scatter.3.cloned.1.call-start = ((), (), s32[]{:S(2)}) async-start(), calls=%async_computation.2 | async-start | bytes 2228224 | tf_op jit(solution)/shard_map/reduce_scatter | solution.py:45
  8.0 5.5 copy-start.2
  9.6 3.8 copy-start.1
  13.5 10.5 %copy-start.3 = (f32[1024,256]{1,0:T(8,128)S(1)}, f32[1024,256]{1,0:T(8,128)}, u32[]{:S(2)}) copy-start(f32[1024,256]{1,0:T(8,128)} %param.12) | copy-start | bytes 3145732
  23.8 146.2 %reduce-scatter.5.cloned.1.call-start = ((), (), s32[]{:S(2)}) async-start(), calls=%async_computation.3 | async-start | bytes 2228224 | tf_op jit(solution)/shard_map/reduce_scatter | solution.py:45
  24.0 14.3 %copy-start.10 = (s32[64]{0:T(128)S(1)}, s32[64]{0:T(128)}, u32[]{:S(2)}) copy-start(s32[64]{0:T(128)} %param.14) | copy-start | bytes 772
  24.0 14.3 %copy-start.11 = (s32[64]{0:T(128)S(1)}, s32[64]{0:T(128)}, u32[]{:S(2)}) copy-start(s32[64]{0:T(128)} %param.13) | copy-start | bytes 772
  24.1 520.2 %copy-start.8 = (f32[256,256]{1,0:T(8,128)S(1)}, f32[256,256]{1,0:T(8,128)}, u32[]{:S(2)}) copy-start(f32[256,256]{1,0:T(8,128)} %param.16) | copy-start | bytes 786436
  36.9 509.8 %copy-start.9 = (f32[256,256]{1,0:T(8,128)S(1)}, f32[256,256]{1,0:T(8,128)}, u32[]{:S(2)}) copy-start(f32[256,256]{1,0:T(8,128)} %param.17) | copy-start | bytes 786436
  37.0 246.6 %all-gather.5.cloned.1.call-start = ((), (), s32[]{:S(2)}) async-start(), calls=%async_computation.5 | async-start | bytes 17825792 | tf_op jit(solution)/shard_map/all_gather | solution.py:41
  37.7 355.5 %all-gather.3.cloned.1.call-start = ((), (), s32[]{:S(2)}) async-start(), calls=%async_computation.4 | async-start | bytes 17825792 | tf_op jit(solution)/shard_map/all_gather | solution.py:41
  38.3 506.0 %all-reduce.3.cloned.1.call-start = ((), (), s32[]{:S(2)}) async-start(), calls=%async_computation.6 | async-start | bytes 1572864 | tf_op jit(solution)/shard_map/psum | solution.py:54
  97.0 452.1 %copy-start.4 = (f32[128,256]{1,0:T(8,128)}, f32[128,256]{1,0:T(8,128)S(1)}, u32[]{:S(2)}) copy-start(f32[128,256]{1,0:T(8,128)S(1)} %neg.9) | copy-start | bytes 393220
  171.2 377.9 %copy-start.7 = (f32[128,256]{1,0:T(8,128)}, f32[128,256]{1,0:T(8,128)S(1)}, u32[]{:S(2)}) copy-start(f32[128,256]{1,0:T(8,128)S(1)} %fusion.4) | copy-start | bytes 393220
  545.2 3.8 copy-start.5
  546.7 2.4 copy-start.6
Sparse Core Ops, SparseCore 0:
  23.9 72.0 reduce-scatter.2
  100.0 69.9 reduce-scatter.4
  172.4 111.1 all-gather.4
  285.8 107.4 all-gather.2
  398.7 145.5 all-reduce.2
where the time goes:
time: 556 us
  waiting for transfers between devices  499 us (90%)
  matrix products  34.3 us (6%)
  between operations  14 us (3%)
    all_gather x2, waiting for transfers between devices, fetch_rows(): gathered = lax.all_gather(factor, 'col', axis=0, tiled=True)  218 us
    psum x1, waiting for transfers between devices, per_device(): lax.psum(jnp.dot(near_one.T, panel_one, precision=high), ('row', 'col'))  149 us
    reduce_scatter x2, waiting for transfers between devices, panel_product(): lax.psum_scatter(jnp.dot(masked, factor_kept, precision=high), 'col', sca...  131 us
    dot_general x2, matrix products, panel_product(): jnp.dot(masked, factor_kept, precision=high)  23.1 us
  transfers between devices with their start and end apart: 5, of which 5 were waited for; matrix products, arithmetic and copies ran while one was open for 3% of the time, Pallas kernels for 0%

commit v1 on v0

--- a/solution.py
+++ b/solution.py
@@ -51,7 +51,7 @@
     panel_one = -panel_product(x_one)
     near_one = fetch_rows(factor_first)
     near_one = near_one * member(own_ids, rows_first)[:, None]
-    first_total = lax.psum(jnp.dot(near_one.T, panel_one, precision=high), ("row", "col"))
+    first_total = lax.psum(lax.psum(jnp.dot(near_one.T, panel_one, precision=high), "row"), "col")
     block_one = diag_first - first_total
     near_two = fetch_rows(factor_second)
     near_two = near_two * member(own_ids, rows_second)[:, None]

time: 556 us -> 773 us (1.39)
  waiting for transfers between devices: 499 us -> 715 us
    psum x1 -> x3, waiting for transfers between devices: 149 us -> 359 us  [the longest x1 152 us: per_device(): lax.psum((jnp.dot(panel_one.T, near_two, precision=high), jnp.dot(near_tw...]
    all_gather x2, waiting for transfers between devices: 218 us -> 229 us  [fetch_rows(): gathered = lax.all_gather(factor, 'col', axis=0, tiled=True)]
  transfers between devices with their start and end apart: 5 -> 7, of which waited for: 5 -> 7; matrix products, arithmetic and copies ran while one was open for 3% -> 3% of each run, Pallas kernels for 0% -> 0%
where the time goes in v1:
time: 773 us
  waiting for transfers between devices  715 us (92%)
  matrix products  34.1 us (4%)
  between operations  14.3 us (2%)
    all_gather x2, waiting for transfers between devices, fetch_rows(): gathered = lax.all_gather(factor, 'col', axis=0, tiled=True)  229 us
    psum x1, waiting for transfers between devices, per_device(): lax.psum((jnp.dot(panel_one.T, near_two, precision=high), jnp.dot(near_tw...  152 us
    psum x1, waiting for transfers between devices, per_device(): lax.psum(lax.psum(jnp.dot(near_one.T, panel_one, precision=high), 'row'),...  134 us
    reduce_scatter x2, waiting for transfers between devices, panel_product(): lax.psum_scatter(jnp.dot(masked, factor_kept, precision=high), 'col', sca...  126 us
    psum x1, waiting for transfers between devices, per_device(): lax.psum(jnp.dot(near_one.T, panel_one, precision=high), 'row')  72.5 us
    dot_general x2, matrix products, panel_product(): jnp.dot(masked, factor_kept, precision=high)  23.1 us
  transfers between devices with their start and end apart: 7, of which 7 were waited for; matrix products, arithmetic and copies ran while one was open for 3% of the time, Pallas kernels for 0%

profile of v1, /device:TPU:1, one launch (start us, length us, event | category | flops | bytes accessed | tf_op | source)
XLA Modules:
  0.0 772.5 jit_solution(7169947626777198687)
XLA Ops:
  7.2 0.0 copy-start
  7.2 0.0 reduce-scatter.3.cloned.1.call-start
  7.2 0.7 convert_element_type.15
  8.0 0.1 copy.16
  8.0 0.0 copy-start.2
  8.0 1.0 convert_reduce_fusion
  9.0 0.6 mul.52
  9.6 0.0 copy-start.1
  9.6 3.8 copy-done.1
  13.4 0.1 copy-done.2
  13.5 0.0 copy-start.3
  13.5 10.3 %fusion.1 = f32[2048,256]{1,0:T(8,128)} fusion(f32[2048,1024]{1,0:T(8,128)S(1)} %copy-done.2, f32[256,8,8,128]{3,2,1,0:T(8,128)S(1)} %bitcast.19, f32[1024,256]{1,0:T(8,128)} %param.11, f32[1024]{0:T(1024)S(1)} %get-tuple-element.6), kind=kOutput, calls=%fused_computation.2 | convolution fusion | flops 6444810240 | bytes 19927040 | tf_op jit(solution)/shard_map/dot_general | solution.py:46
  23.8 0.0 reduce-scatter.3.cloned.1.call-update
  23.8 0.0 all-gather.3.cloned.1.call-start
  23.8 0.7 all-gather.3.cloned.1.call-update
  24.5 0.2 reduce-scatter.5.cloned.1.call-start
  24.8 0.0 copy-done.3
  24.8 0.0 copy-start.10
  24.8 0.0 copy-start.11
  24.8 0.0 copy-start.8
  24.8 12.8 %fusion = f32[2048,256]{1,0:T(8,128)} fusion(f32[2048,1024]{1,0:T(8,128)} %param.9, f32[256,8,8,128]{3,2,1,0:T(8,128)} %bitcast.20, f32[1024,256]{1,0:T(8,128)S(1)} %copy-done.3, f32[1024]{0:T(1024)S(1)} %get-tuple-element.5), kind=kOutput, calls=%fused_computation.1 | convolution fusion | flops 6444810240 | bytes 19927040 | tf_op jit(solution)/shard_map/dot_general | solution.py:46
  37.6 0.0 copy-start.9
  37.6 0.0 reduce-scatter.5.cloned.1.call-update
  37.6 0.0 all-reduce.5.cloned.1.call-start
  37.7 0.0 copy-done.10
  37.7 0.0 copy-done.11
  37.7 0.1 convert_reduce_fusion.2
  37.8 58.2 %reduce-scatter.3.cloned.1.call-done = f32[128,256]{1,0:T(8,128)} async-done(((f32[2048,256]{1,0:T(8,128)}), f32[128,256]{1,0:T(8,128)}) %reduce-scatter.3.cloned.1.call-update) | async-done | bytes 131088 | tf_op jit(solution)/shard_map/reduce_scatter | solution.py:45
  96.0 0.9 neg.9
  96.9 0.0 copy-start.4
  96.9 112.6 %all-gather.3.cloned.1.call-done = f32[16384,256]{1,0:T(8,128)} async-done(((f32[1024,256]{1,0:T(8,128)}), f32[16384,256]{1,0:T(8,128)}) %all-gather.3.cloned.1.call-update) | async-done | bytes 16777232 | tf_op jit(solution)/shard_map/all_gather | solution.py:41
  209.6 2.1 fusion.9
  211.7 0.0 all-reduce.5.cloned.1.call-update
  211.7 0.0 all-gather.5.cloned.1.call-start
  211.7 0.5 all-gather.5.cloned.1.call-update
  212.3 0.0 all-reduce.7.cloned.1.call-start
  212.3 67.4 %reduce-scatter.5.cloned.1.call-done = f32[128,256]{1,0:T(8,128)} async-done(((f32[2048,256]{1,0:T(8,128)}), f32[128,256]{1,0:T(8,128)}) %reduce-scatter.5.cloned.1.call-update) | async-done | bytes 131088 | tf_op jit(solution)/shard_map/reduce_scatter | solution.py:45
  279.8 0.0 copy-done
  279.8 1.2 fusion.4
  281.0 0.0 copy-start.7
  281.0 72.5 %all-reduce.5.cloned.1.call-done = f32[256,256]{1,0:T(8,128)} async-done(((f32[256,256]{1,0:T(8,128)}), f32[256,256]{1,0:T(8,128)}) %all-reduce.5.cloned.1.call-update) | async-done | bytes 262160 | tf_op jit(solution)/shard_map/psum | solution.py:54
  353.4 0.0 all-reduce.7.cloned.1.call-update
  353.4 0.0 all-reduce.9.cloned.1.call-start
  353.5 116.7 %all-gather.5.cloned.1.call-done = f32[16384,256]{1,0:T(8,128)} async-done(((f32[1024,256]{1,0:T(8,128)}), f32[16384,256]{1,0:T(8,128)}) %all-gather.5.cloned.1.call-update) | async-done | bytes 16777232 | tf_op jit(solution)/shard_map/all_gather | solution.py:41
  470.2 2.1 fusion.13
  472.2 2.1 fusion.12
  474.3 0.0 all-reduce.9.cloned.1.call-update
  474.3 134.2 %all-reduce.7.cloned.1.call-done = f32[256,256]{1,0:T(8,128)} async-done(((f32[256,256]{1,0:T(8,128)}), f32[256,256]{1,0:T(8,128)}) %all-reduce.7.cloned.1.call-update) | async-done | bytes 262160 | tf_op jit(solution)/shard_map/psum | solution.py:54
  608.5 0.0 copy-done.8
  608.5 1.0 sub.23
  609.5 0.0 copy-start.5
  609.5 152.4 %all-reduce.9.cloned.1.call-done = (f32[256,256]{1,0:T(8,128)}, f32[256,256]{1,0:T(8,128)}) async-done(((f32[256,256]{1,0:T(8,128)}, f32[256,256]{1,0:T(8,128)}), (f32[256,256]{1,0:T(8,128)}, f32[256,256]{1,0:T(8,128)})) %all-reduce.9.cloned.1.call-update) | async-done | bytes 524304 | tf_op jit(solution)/shard_map/psum | solution.py:59
  761.9 1.3 fusion.3
  763.3 0.0 copy-start.6
  763.3 0.0 copy-done.9
  763.3 2.3 fusion.2
  765.6 0.0 copy-done.4
  765.6 0.0 copy-done.7
  765.6 0.0 copy-done.5
  765.7 0.0 copy-done.6
  (2 shorter events, 0.0 us)
Async XLA Ops:
  7.2 272.6 %copy-start = (f32[256,256]{1,0:T(8,128)S(1)}, f32[256,256]{1,0:T(8,128)}, u32[]{:S(2)}) copy-start(f32[256,256]{1,0:T(8,128)} %param.15) | copy-start | bytes 786436
  7.2 88.8 %reduce-scatter.3.cloned.1.call-start = ((), (), s32[]{:S(2)}) async-start(), calls=%async_computation.2 | async-start | bytes 2228224 | tf_op jit(solution)/shard_map/reduce_scatter | solution.py:45
  8.0 5.5 copy-start.2
  9.6 3.8 copy-start.1
  13.5 11.3 %copy-start.3 = (f32[1024,256]{1,0:T(8,128)S(1)}, f32[1024,256]{1,0:T(8,128)}, u32[]{:S(2)}) copy-start(f32[1024,256]{1,0:T(8,128)} %param.12) | copy-start | bytes 3145732
  23.8 185.8 %all-gather.3.cloned.1.call-start = ((), (), s32[]{:S(2)}) async-start(), calls=%async_computation.4 | async-start | bytes 17825792 | tf_op jit(solution)/shard_map/all_gather | solution.py:41
  24.5 255.2 %reduce-scatter.5.cloned.1.call-start = ((), (), s32[]{:S(2)}) async-start(), calls=%async_computation.3 | async-start | bytes 2228224 | tf_op jit(solution)/shard_map/reduce_scatter | solution.py:45
  24.8 12.9 %copy-start.10 = (s32[64]{0:T(128)S(1)}, s32[64]{0:T(128)}, u32[]{:S(2)}) copy-start(s32[64]{0:T(128)} %param.14) | copy-start | bytes 772
  24.8 12.9 %copy-start.11 = (s32[64]{0:T(128)S(1)}, s32[64]{0:T(128)}, u32[]{:S(2)}) copy-start(s32[64]{0:T(128)} %param.13) | copy-start | bytes 772
  24.8 583.7 %copy-start.8 = (f32[256,256]{1,0:T(8,128)S(1)}, f32[256,256]{1,0:T(8,128)}, u32[]{:S(2)}) copy-start(f32[256,256]{1,0:T(8,128)} %param.16) | copy-start | bytes 786436
  37.6 725.7 %copy-start.9 = (f32[256,256]{1,0:T(8,128)S(1)}, f32[256,256]{1,0:T(8,128)}, u32[]{:S(2)}) copy-start(f32[256,256]{1,0:T(8,128)} %param.17) | copy-start | bytes 786436
  37.6 315.8 %all-reduce.5.cloned.1.call-start = ((), (), s32[]{:S(2)}) async-start(), calls=%async_computation.5 | async-start | bytes 524288 | tf_op jit(solution)/shard_map/psum | solution.py:54
  96.9 668.7 %copy-start.4 = (f32[128,256]{1,0:T(8,128)}, f32[128,256]{1,0:T(8,128)S(1)}, u32[]{:S(2)}) copy-start(f32[128,256]{1,0:T(8,128)S(1)} %neg.9) | copy-start | bytes 393220
  211.7 258.5 %all-gather.5.cloned.1.call-start = ((), (), s32[]{:S(2)}) async-start(), calls=%async_computation.7 | async-start | bytes 17825792 | tf_op jit(solution)/shard_map/all_gather | solution.py:41
  212.3 396.2 %all-reduce.7.cloned.1.call-start = ((), (), s32[]{:S(2)}) async-start(), calls=%async_computation.6 | async-start | bytes 524288 | tf_op jit(solution)/shard_map/psum | solution.py:54
  281.0 484.7 %copy-start.7 = (f32[128,256]{1,0:T(8,128)}, f32[128,256]{1,0:T(8,128)S(1)}, u32[]{:S(2)}) copy-start(f32[128,256]{1,0:T(8,128)S(1)} %fusion.4) | copy-start | bytes 393220
  353.4 408.5 %all-reduce.9.cloned.1.call-start = ((), (), s32[]{:S(2)}) async-start(), calls=%async_computation.8 | async-start | bytes 1048576 | tf_op jit(solution)/shard_map/psum | solution.py:59
  609.5 156.2 %copy-start.5 = (f32[256,256]{1,0:T(8,128)}, f32[256,256]{1,0:T(8,128)S(1)}, u32[]{:S(2)}) copy-start(f32[256,256]{1,0:T(8,128)S(1)} %sub.23) | copy-start | bytes 786436
  763.3 2.4 copy-start.6
Sparse Core Ops, SparseCore 0:
  23.9 72.0 reduce-scatter.2
  98.4 111.1 all-gather.2
  213.5 66.1 reduce-scatter.4
  282.7 70.7 all-reduce.4
  355.7 114.4 all-gather.4
  472.5 135.9 all-reduce.6
  614.0 147.8 all-reduce.8
